TPU v7x, 32 devices: a whole 2x2x4 slice. The times are simulated.
32 devices in a mesh: dp: 8 (over z, x), mlp: 4 (over y, core).
Axes of the slice: x: 2, y: 2, z: 4, core: 2. Of those that a mesh axis runs over, the one named last changes fastest.
Arguments:
- tokens: bfloat16 [32768, 768], P(('dp', 'mlp')), may hold values from -6 to 6
- cotangent: bfloat16 [32768, 768], P(('dp', 'mlp')), may hold values from -6 to 6
- vectors: float32 [14, 768], replicated
- vector_moments: float32 [14, 768], replicated, may hold values from 819.2 to 26214.4
- decays: float32 [2], replicated, may hold values from 0.9 to 0.98
- owner: int32 [4, 3], replicated, may hold values from 0 to 7, as said below
- master_slots: float32 [8, 4, 768, 768], P('dp', 'mlp'), as said below
- left_slots: float32 [8, 4, 768, 768], P('dp', 'mlp'), as said below
- right_slots: float32 [8, 4, 768, 768], P('dp', 'mlp'), as said below
- left_roots: float32 [8, 4, 768, 768], P('dp', 'mlp'), as said below
- right_roots: float32 [8, 4, 768, 768], P('dp', 'mlp'), as said below
- grid_height: int32 [128], P(('dp', 'mlp')), may hold values from 8 to 24, as said below
- grid_width: int32 [128], P(('dp', 'mlp')), may hold values from 8 to 24, as said below
- patch_rows: int32 [32768], P(('dp', 'mlp')), may hold values from 0 to 23, as said below
- patch_cols: int32 [32768], P(('dp', 'mlp')), may hold values from 0 to 23, as said below
- segment: int32 [32768], P(('dp', 'mlp')), may hold values from 0 to 3, as said below
Outputs:
- output: bfloat16 [32768, 768], P(('dp', 'mlp'))
- input_grad: float32 [32768, 768], P(('dp', 'mlp'))
- slot_grads: float32 [8, 4, 768, 768], P('dp', 'mlp')
- new_left: float32 [8, 4, 768, 768], P('dp', 'mlp')
- new_right: float32 [8, 4, 768, 768], P('dp', 'mlp')
- new_master: float32 [8, 4, 768, 768], P('dp', 'mlp')
- vector_grads: float32 [14, 768], P(None, 'mlp')
- new_vector_moments: float32 [14, 768], P(None, 'mlp')
- new_vectors: float32 [14, 768], P(None, 'mlp')
Inputs may be any that keep to these rules, and one draw needn't show every extreme that they name: `owner`: the entries of a row differ; block kind 0 of row m is the m-th of the query, key, value and output projections, kind 1 the m-th 768 columns of the up projection, kind 2 the m-th 768 rows of the down projection. `master_slots`: slot (owner[m,k], m) holds block kind k of row m; the other slots are unused. `left_slots`: symmetric and positive definite. `right_slots`: symmetric and positive definite. `left_roots`: symmetric and positive definite. `right_roots`: symmetric and positive definite. `grid_height`: each image is 16 patches along one side; the other sides of one device's images add up to 64. `grid_width`: as grid_height. `patch_rows`: each device's patches hold its images whole, one after another in the order of their numbers, each in raster order. `patch_cols`: as patch_rows. `segment`: never falls within a device's patches.
All inputs are finite; a program needn't handle non-finite values.
Results may differ from a plain program's by a relative error of at most 0.014.
Values may be sent and summed in bfloat16 or wider, within the bound.
A program may use at most 192 MiB of HBM per device.

v0:
```python
import math
import jax
import jax.numpy as jnp
from jax import lax
from jax.sharding import PartitionSpec as P

HEADS = 12
GRID_BASE = 16
NORM_EPSILON = 1e-06
GRAFT_EPSILON = 1e-06
STEP_EPSILON = 1e-08
RATE_MATRIX = 0.04
RATE_VECTOR = 0.02
MASKED_SCORE = -1e30


def layer_norm(values, gain_row, shift_row):
    centred = values - jnp.mean(values, axis=-1, keepdims=True)
    spread = jnp.mean(centred * centred, axis=-1, keepdims=True)
    return centred * lax.rsqrt(spread + NORM_EPSILON) * gain_row + shift_row


def exact_gelu(values):
    return jax.nn.gelu(values, approximate=False)


def rotate_pairs(flat_values, freq_row, rows_pos, cols_pos):
    tokens_here = flat_values.shape[0]
    values = flat_values.reshape(tokens_here, HEADS, -1)
    half_size = values.shape[-1] // 2
    middle = freq_row.shape[0] // 2
    freq_cols = freq_row[:middle].reshape(HEADS, half_size)
    freq_rows = freq_row[middle:].reshape(HEADS, half_size)
    angle_grid = (
        rows_pos[:, None, None] * freq_rows[None] + cols_pos[:, None, None] * freq_cols[None]
    )
    cosine = jnp.cos(angle_grid)
    sine_part = jnp.sin(angle_grid)
    first_half = values[..., :half_size]
    second = values[..., half_size:]
    turned = jnp.concatenate(
        [first_half * cosine - second * sine_part, second * cosine + first_half * sine_part],
        axis=-1,
    )
    return turned.reshape(tokens_here, -1)


def patch_positions(segment_ids, heights_in, widths_in, rows_in, cols_in):
    images_here = heights_in.shape[0]
    matches = segment_ids[:, None] == jnp.arange(images_here, dtype=jnp.int32)[None, :]
    heights = jnp.sum(jnp.where(matches, heights_in[None, :], 0), axis=1).astype(jnp.float32)
    widths = jnp.sum(jnp.where(matches, widths_in[None, :], 0), axis=1).astype(jnp.float32)
    rows_pos = rows_in.astype(jnp.float32) * GRID_BASE / heights
    cols_pos = cols_in.astype(jnp.float32) * GRID_BASE / widths
    return (rows_pos, cols_pos)


def heads_first(flat_values):
    return jnp.swapaxes(flat_values.reshape(flat_values.shape[0], HEADS, -1), 0, 1)


def tokens_first(stacked):
    return jnp.swapaxes(stacked, 0, 1).reshape(stacked.shape[1], -1)


def local(
    tokens,
    cotangent,
    vectors,
    vector_moments,
    decays,
    owner,
    master_slots,
    left_slots,
    right_slots,
    left_roots,
    right_roots,
    grid_height,
    grid_width,
    patch_rows,
    patch_cols,
    segment,
):
    dp_index = lax.axis_index("dp")
    mlp_index = lax.axis_index("mlp")
    groups_mlp = lax.axis_size("mlp")
    model_width = tokens.shape[1]
    rows_here = tokens.shape[0]
    owner_row = jnp.take(owner, mlp_index, axis=0)
    holds_block = owner_row == dp_index
    owned_blocks = jnp.where(holds_block[:, None, None], master_slots[0, 0][None], 0.0)
    blocks = lax.psum(owned_blocks, "dp")
    blocks_low = blocks.astype(jnp.bfloat16)
    up_rows = vectors[8 : 8 + groups_mlp]
    down_bias = vectors[8 + groups_mlp]
    freq_row = vectors[9 + groups_mlp]
    every_block = lax.all_gather(blocks_low[None], "mlp", axis=0, tiled=True)
    attention_weights = every_block[:, 0]
    up_weight = every_block[:, 1]
    down_weight = every_block[:, 2]
    up_bias = up_rows.reshape(-1)
    inputs = tokens.astype(jnp.float32)
    norm_one, norm_one_back = jax.vjp(layer_norm, inputs, vectors[0], vectors[1])
    norm_one_low = norm_one.astype(jnp.bfloat16)
    query_lin = (
        jnp.dot(norm_one_low, attention_weights[0], preferred_element_type=jnp.float32) + vectors[2]
    )
    key_lin = (
        jnp.dot(norm_one_low, attention_weights[1], preferred_element_type=jnp.float32) + vectors[3]
    )
    value_low = (
        jnp.dot(norm_one_low, attention_weights[2], preferred_element_type=jnp.float32) + vectors[4]
    ).astype(jnp.bfloat16)
    rows_pos, cols_pos = patch_positions(segment, grid_height, grid_width, patch_rows, patch_cols)

    def rotary_map(flat_values, freq_values):
        return rotate_pairs(flat_values, freq_values, rows_pos, cols_pos)

    query_rot, query_back = jax.vjp(rotary_map, query_lin, freq_row)
    key_rot, key_back = jax.vjp(rotary_map, key_lin, freq_row)
    query_heads = heads_first(query_rot.astype(jnp.bfloat16))
    key_heads = heads_first(key_rot.astype(jnp.bfloat16))
    value_heads = heads_first(value_low)
    same_image = segment[:, None] == segment[None, :]
    score_scale = 1.0 / math.sqrt(model_width // HEADS)

    def head_scores(query_head, key_head):
        scores = jnp.dot(query_head, key_head.T, preferred_element_type=jnp.float32) * score_scale
        return jnp.where(same_image, scores, MASKED_SCORE)

    def head_forward(pieces):
        query_head, key_head, value_head = pieces
        scores = head_scores(query_head, key_head)
        row_peak = jnp.max(scores, axis=1, keepdims=True)
        exponent = jnp.exp(scores - row_peak)
        row_total = jnp.sum(exponent, axis=1, keepdims=True)
        weights_low = (exponent / row_total).astype(jnp.bfloat16)
        attended = jnp.dot(weights_low, value_head, preferred_element_type=jnp.float32)
        return (attended, (row_peak + jnp.log(row_total))[:, 0])

    attended_heads, log_totals = lax.map(head_forward, (query_heads, key_heads, value_heads))
    attended_low = tokens_first(attended_heads).astype(jnp.bfloat16)
    branch_one = (
        jnp.dot(attended_low, attention_weights[3], preferred_element_type=jnp.float32) + vectors[5]
    )
    middle = inputs + branch_one
    norm_two, norm_two_back = jax.vjp(layer_norm, middle, vectors[6], vectors[7])
    norm_two_low = norm_two.astype(jnp.bfloat16)
    pre_act = (
        jnp.einsum(
            "td,mde->tme", norm_two_low, up_weight, preferred_element_type=jnp.float32
        ).reshape(rows_here, -1)
        + up_bias
    )
    activation, gelu_back = jax.vjp(exact_gelu, pre_act)
    activation_blocks = activation.astype(jnp.bfloat16).reshape(rows_here, groups_mlp, -1)
    branch_two = (
        jnp.einsum(
            "tme,med->td", activation_blocks, down_weight, preferred_element_type=jnp.float32
        )
        + down_bias
    )
    grad_act = jnp.einsum(
        "td,med->tme", cotangent, down_weight, preferred_element_type=jnp.float32
    ).reshape(rows_here, -1)
    grad_down = jnp.einsum(
        "tme,td->med", activation_blocks, cotangent, preferred_element_type=jnp.float32
    )
    grad_pre_blocks = gelu_back(grad_act)[0].astype(jnp.bfloat16).reshape(rows_here, groups_mlp, -1)
    grad_up = jnp.einsum(
        "td,tme->mde", norm_two_low, grad_pre_blocks, preferred_element_type=jnp.float32
    )
    up_grad_rows = jnp.sum(grad_pre_blocks, axis=0, dtype=jnp.float32)
    grad_norm_two = jnp.einsum(
        "tme,mde->td", grad_pre_blocks, up_weight, preferred_element_type=jnp.float32
    )
    output_low = (middle + branch_two).astype(jnp.bfloat16)
    grad_middle_norm, grad_gain_two, grad_shift_two = norm_two_back(grad_norm_two)
    grad_middle = cotangent.astype(jnp.float32) + grad_middle_norm
    grad_branch_low = grad_middle.astype(jnp.bfloat16)
    grad_out_bias = jnp.sum(grad_branch_low, axis=0, dtype=jnp.float32)
    grad_out_weight = jnp.dot(attended_low.T, grad_branch_low, preferred_element_type=jnp.float32)
    grad_attended_low = jnp.dot(
        grad_branch_low, attention_weights[3].T, preferred_element_type=jnp.float32
    ).astype(jnp.bfloat16)

    def head_backward(pieces):
        query_head, key_head, value_head, grad_head, log_total = pieces
        scores = head_scores(query_head, key_head)
        probs = jnp.exp(scores - log_total[:, None])
        grad_probs = jnp.dot(grad_head, value_head.T, preferred_element_type=jnp.float32)
        inner = jnp.sum(probs * grad_probs, axis=1, keepdims=True)
        grad_scores = (probs * (grad_probs - inner)).astype(jnp.bfloat16)
        grad_query = (
            jnp.dot(grad_scores, key_head, preferred_element_type=jnp.float32) * score_scale
        )
        grad_key = (
            jnp.dot(grad_scores.T, query_head, preferred_element_type=jnp.float32) * score_scale
        )
        grad_value = jnp.dot(
            probs.astype(jnp.bfloat16).T, grad_head, preferred_element_type=jnp.float32
        )
        return (grad_query, grad_key, grad_value)

    grad_queries, grad_keys, grad_values = lax.map(
        head_backward,
        (query_heads, key_heads, value_heads, heads_first(grad_attended_low), log_totals),
    )
    grad_query_lin, grad_freq_query = query_back(tokens_first(grad_queries))
    grad_key_lin, grad_freq_key = key_back(tokens_first(grad_keys))
    grad_query_low = grad_query_lin.astype(jnp.bfloat16)
    grad_key_low = grad_key_lin.astype(jnp.bfloat16)
    grad_value_low = tokens_first(grad_values).astype(jnp.bfloat16)
    grad_query_weight = jnp.dot(norm_one_low.T, grad_query_low, preferred_element_type=jnp.float32)
    grad_key_weight = jnp.dot(norm_one_low.T, grad_key_low, preferred_element_type=jnp.float32)
    grad_value_weight = jnp.dot(norm_one_low.T, grad_value_low, preferred_element_type=jnp.float32)
    grad_norm_one = jnp.dot(
        grad_query_low, attention_weights[0].T, preferred_element_type=jnp.float32
    )
    grad_norm_one = grad_norm_one + jnp.dot(
        grad_key_low, attention_weights[1].T, preferred_element_type=jnp.float32
    )
    grad_norm_one = grad_norm_one + jnp.dot(
        grad_value_low, attention_weights[2].T, preferred_element_type=jnp.float32
    )
    grad_input_norm, grad_gain_one, grad_shift_one = norm_one_back(grad_norm_one)
    input_grad = grad_middle + grad_input_norm
    head_rows = jnp.stack(
        [
            grad_gain_one,
            grad_shift_one,
            jnp.sum(grad_query_low, axis=0, dtype=jnp.float32),
            jnp.sum(grad_key_low, axis=0, dtype=jnp.float32),
            jnp.sum(grad_value_low, axis=0, dtype=jnp.float32),
            grad_out_bias,
            grad_gain_two,
            grad_shift_two,
        ]
    )
    tail_rows = jnp.stack(
        [jnp.sum(cotangent, axis=0, dtype=jnp.float32), grad_freq_query + grad_freq_key]
    )
    local_vectors = jnp.concatenate([head_rows, up_grad_rows, tail_rows], axis=0)
    vector_sum = lax.psum(local_vectors, ("dp", "mlp"))
    attention_grads = jnp.stack(
        [grad_query_weight, grad_key_weight, grad_value_weight, grad_out_weight]
    )
    attention_share, up_share, down_share = (
        lax.psum_scatter(
            attention_grads.astype(jnp.bfloat16), "mlp", scatter_dimension=0, tiled=True
        ).astype(jnp.float32),
        lax.psum_scatter(
            grad_up.astype(jnp.bfloat16), "mlp", scatter_dimension=0, tiled=True
        ).astype(jnp.float32),
        lax.psum_scatter(
            grad_down.astype(jnp.bfloat16), "mlp", scatter_dimension=0, tiled=True
        ).astype(jnp.float32),
    )
    grad_stack = jnp.concatenate([attention_share, up_share, down_share], axis=0)
    reduced = lax.psum(grad_stack, "dp")
    block_kind = jnp.sum(jnp.where(holds_block, jnp.arange(3, dtype=jnp.int32), 0))
    owns_block = jnp.any(holds_block)
    gradient = jnp.take(reduced, block_kind, axis=0)
    decay_matrix = decays[0]
    left_old = left_slots[0, 0]
    right_old = right_slots[0, 0]
    master_old = master_slots[0, 0]
    left_next = decay_matrix * left_old + (1.0 - decay_matrix) * jnp.dot(
        gradient, gradient.T, precision=lax.Precision.HIGHEST
    )
    right_next = decay_matrix * right_old + (1.0 - decay_matrix) * jnp.dot(
        gradient.T, gradient, precision=lax.Precision.HIGHEST
    )
    direction = jnp.dot(
        jnp.dot(left_roots[0, 0], gradient, precision=lax.Precision.HIGHEST),
        right_roots[0, 0],
        precision=lax.Precision.HIGHEST,
    )
    normed_step = direction * lax.rsqrt(jnp.mean(direction * direction) + GRAFT_EPSILON)
    master_next = master_old - RATE_MATRIX * normed_step
    slot_grad = jnp.where(owns_block, gradient, 0.0)[None, None]
    left_out = jnp.where(owns_block, left_next, left_old)[None, None]
    right_out = jnp.where(owns_block, right_next, right_old)[None, None]
    master_out = jnp.where(owns_block, master_next, master_old)[None, None]
    share_width = model_width // groups_mlp

    def own_columns(table):
        return lax.dynamic_slice_in_dim(table, mlp_index * share_width, share_width, 1)

    grad_share = own_columns(vector_sum)
    moment_old = own_columns(vector_moments)
    vector_old = own_columns(vectors)
    decay_vector = decays[1]
    moment_next = decay_vector * moment_old + (1.0 - decay_vector) * grad_share * grad_share
    vector_next = vector_old - RATE_VECTOR * grad_share / (jnp.sqrt(moment_next) + STEP_EPSILON)
    return (
        output_low,
        input_grad,
        slot_grad,
        left_out,
        right_out,
        master_out,
        grad_share,
        moment_next,
        vector_next,
    )


def solution(mesh):
    placed = (
        P(("dp", "mlp"), None),
        P(("dp", "mlp"), None),
        P(),
        P(),
        P(),
        P(),
        P("dp", "mlp", None, None),
        P("dp", "mlp", None, None),
        P("dp", "mlp", None, None),
        P("dp", "mlp", None, None),
        P("dp", "mlp", None, None),
        P(("dp", "mlp")),
        P(("dp", "mlp")),
        P(("dp", "mlp")),
        P(("dp", "mlp")),
        P(("dp", "mlp")),
    )
    return jax.shard_map(
        local,
        mesh=mesh,
        in_specs=placed,
        out_specs=(
            P(("dp", "mlp"), None),
            P(("dp", "mlp"), None),
            P("dp", "mlp", None, None),
            P("dp", "mlp", None, None),
            P("dp", "mlp", None, None),
            P("dp", "mlp", None, None),
            P(None, "mlp"),
            P(None, "mlp"),
            P(None, "mlp"),
        ),
        check_vma=False,
    )
```

profile of v0, /device:TPU:0, one launch (start us, length us, event | category | flops | bytes accessed | tf_op | source)
XLA Modules:
  0.0 1202.3 jit_solution(14143546167382789815)
XLA Ops:
  8.8 5.2 broadcast_select_fusion
  14.0 278.3 %all-reduce.12 = bf16[3,768,768]{2,1,0:T(8,128)(2,1)} all-reduce(f32[3,768,768]{2,1,0:T(8,128)} %broadcast_select_fusion), channel_id=1, replica_groups=mesh['dp'=8,'mlp'=4] {'dp'}, use_global_device_ids=true, to_apply=%region_2.3 | all-reduce | flops 1769472 | bytes 10616832 | tf_op jit(solution)/shard_map/psum | solution.py:92
  303.2 78.7 %all-gather.3.cloned.1.call-done = bf16[12,768,768]{2,1,0:T(8,128)(2,1)} async-done(((bf16[3,768,768]{2,1,0:T(8,128)(2,1)}), bf16[12,768,768]{2,1,0:T(8,128)(2,1)}) %all-gather.3.cloned.1.call-update) | async-done | bytes 14155792 | tf_op jit(solution)/shard_map/all_gather | solution.py:97
  381.8 4.9 slice_bitcast_fusion.3
  389.7 3.8 convolution_add_fusion.1
  393.6 7.7 subtract_convert_fusion
  402.5 4.1 copy.102
  409.1 4.1 copy.103
  413.2 4.5 add_convert_fusion.4
  417.7 4.1 copy.101
  421.8 85.7 %while.32 = (s32[]{:T(128)}, bf16[12,1024,64]{1,2,0:T(8,128)(2,1)}, f32[12,1024]{1,0:T(8,128)}, bf16[12,1024,64]{2,1,0:T(8,128)(2,1)}, bf16[12,1024,64]{2,1,0:T(...) while((s32[]{:T(128)}, bf16[12,1024,64]{1,2,0:T(8,128)(2,1)}, ...), condition=%wide.region_8.9_spmd.clone.clone, body=%wide.region_5.8_spmd.clone.sunk.clone | while | flops 284163072 | bytes 13695065 | solution.py:141
  424.6 3.0 fusion.195
  431.7 3.0 fusion.195
  453.2 3.0 fusion.195
  467.4 3.0 fusion.195
  496.0 3.0 fusion.195
  507.5 10.2 fusion.64
  517.7 12.7 %copy.133 = f32[1024,3072]{1,0:T(8,128)} copy(f32[1024,3072]{0,1:T(8,128)} %bitcast.277) | data formatting | bytes 25165824 | tf_op jit(solution)/shard_map/reshape | solution.py:165
  530.3 6.6 copy.105
  537.0 4.0 fusion.140
  544.0 40.9 %convert_reduce_fusion = (f32[3072]{0:T(1024)}, bf16[1024,3072]{1,0:T(8,128)(2,1)}, f32[1024,3072]{1,0:T(8,128)}, f32[1024,3072]{1,0:T(8,128)}) fusion(f32[1024,3072]{1,0:T(8,128)S(1)} %copy-done.14, f32[3072]{0:T(1024)S(1)} %add.236, bf16[3072,768]{1,0:T(8,128)(2,1)} %bitcast.289, f32[1024,768]{0,1:T(8,128)S(1)} %get-tuple-element.370, ...), kind=kOutput, calls=%fused_computation.58 | convolution fusion | flops 5071696896 | bytes 51943424 | tf_op jit(solution)/shard_map/td,mde->tme/dot_general | solution.py:150
  584.9 12.8 %multiply_convert_fusion.1 = bf16[1024,3072]{1,0:T(8,128)(2,1)} fusion(f32[1024,3072]{1,0:T(8,128)} %get-tuple-element.336, f32[1024,3072]{1,0:T(8,128)} %get-tuple-element.371, f32[3072]{0:T(1024)S(1)} %add.236), kind=kLoop, calls=%fused_computation.60 | loop fusion | flops 12582912 | bytes 31469568 | tf_op jit(solution)/shard_map/convert_element_type | solution.py:156
  597.8 8.6 copy.137
  606.4 9.0 convolution_convert_fusion
  618.0 8.8 copy.138
  626.8 9.9 fusion.141
  636.7 3.5 copy.112
  640.2 3.9 multiply_reduce_fusion.1
  647.4 4.4 convolution_convert_fusion.1
  651.8 4.1 copy.113
  655.9 10.4 convert_bitcast_fusion
  667.0 159.3 %while.33 = (s32[]{:T(128)}, f32[12,1024,64]{1,2,0:T(8,128)}, f32[12,1024,64]{1,2,0:T(8,128)}, bf16[12,1024,64]{1,2,0:T(8,128)(2,1)}, bf16[12,1024,64]{2,1,0:T(8...) while((s32[]{:T(128)}, f32[12,1024,64]{1,2,0:T(8,128)}, ...), condition=%wide.region_15.16_spmd.clone.clone, body=%wide.region_13.15_spmd.clone.sunk.clone | while | flops 681704448 | bytes 34112624 | solution.py:205
  826.3 12.0 multiply_add_fusion.1
  840.7 7.8 multiply_add_fusion
  860.6 48.4 %reduce-scatter.4.cloned.1.call-done = bf16[1,768,768]{2,1,0:T(8,128)(2,1)} async-done(((bf16[4,768,768]{2,1,0:T(8,128)(2,1)}), bf16[1,768,768]{2,1,0:T(8,128)(2,1)}) %reduce-scatter.4.cloned.1.call-update) | async-done | bytes 1179664 | tf_op jit(solution)/shard_map/reduce_scatter | solution.py:249
  909.0 5.3 maximum_convert_fusion
  919.4 10.5 fusion.75
  932.5 3.3 fusion.114
  938.6 3.1 fusion.133
  944.2 3.3 convert_reduce_fusion.2
  947.5 3.6 copy.125
  955.9 45.1 %psum.23 = f32[14,768]{1,0:T(8,128)S(1)} all-reduce(f32[14,768]{1,0:T(8,128)S(1)} %concatenate.21), channel_id=1, replica_groups=mesh['dp'=8,'mlp'=4] {'dp','mlp'}, use_global_device_ids=true, to_apply=%region_39.40 | all-reduce | flops 10752 | bytes 86016 | tf_op jit(solution)/shard_map/psum | solution.py:244
  1003.1 143.9 %all-reduce.11.cloned.1.call-done = f32[3,768,768]{2,1,0:T(8,128)} async-done(((f32[3,768,768]{2,1,0:T(8,128)}), f32[3,768,768]{2,1,0:T(8,128)}) %all-reduce.11.cloned.1.call-update) | async-done | bytes 7077904 | tf_op jit(solution)/shard_map/psum | solution.py:260
  1147.1 13.6 %fusion.79 = f32[768,768]{1,0:T(8,128)S(1)} fusion(f32[1,1,768,768]{3,2,1,0:T(8,128)} %param.29, f32[3,768,768]{2,1,0:T(8,128)} %all-reduce.11.cloned.1.call-done, s32[]{:T(128)S(6)} %select_n.95, pred[]{:T(512)S(6)} %and.13), kind=kOutput, calls=%fused_computation.124 | convolution fusion | flops 5436407808 | bytes 7077893 | tf_op jit(solution)/shard_map/dot_general | solution.py:275
  1160.7 8.7 multiply_reduce_fusion.4
  1170.1 5.0 fusion.76
  1177.5 8.9 fusion.84
  1186.4 9.2 fusion.82
  (331 shorter events, 291.6 us)
Async XLA Ops:
  7.2 1153.5 %copy-start = (f32[1,1,768,768]{3,2,1,0:T(8,128)S(1)}, f32[1,1,768,768]{3,2,1,0:T(8,128)}, u32[]{:S(2)}) copy-start(f32[1,1,768,768]{3,2,1,0:T(8,128)} %param.30) | copy-start | bytes 7077892
  7.2 374.6 %all-gather.3.cloned.1.call-start = ((), (), s32[]{:S(2)}) async-start(), calls=%async_computation.7 | async-start | bytes 17694720 | tf_op jit(solution)/shard_map/all_gather | solution.py:97
  292.3 568.3 %reduce-scatter.8.cloned.1.call-start = ((), (), s32[]{:S(2)}) async-start(), calls=%async_computation.5 | async-start | bytes 5898240 | tf_op jit(solution)/shard_map/reduce_scatter | solution.py:255
  293.7 3.8 copy-start.38
  293.7 4.0 slice-start
  293.7 4.0 copy-start.20
  293.7 4.0 copy-start.53
  293.7 4.0 copy-start.54
  294.8 8.3 copy-start.50
  294.8 8.3 copy-start.51
  297.5 96.0 %copy-start.28 = (f32[12,32]{1,0:T(8,128)}, f32[12,32]{1,0:T(8,128)S(1)}, u32[]{:S(2)}) copy-start(f32[12,32]{1,0:T(8,128)S(1)} %mul.390) | copy-start | bytes 4612
  297.6 95.9 %copy-start.30 = (f32[12,32]{1,0:T(8,128)}, f32[12,32]{1,0:T(8,128)S(1)}, u32[]{:S(2)}) copy-start(f32[12,32]{1,0:T(8,128)S(1)} %mul.385) | copy-start | bytes 4612
  298.4 114.8 %copy-start.40 = (f32[768]{0:T(1024)}, f32[768]{0:T(1024)S(1)}, u32[]{:S(2)}) copy-start(f32[768]{0:T(1024)S(1)} %get-tuple-element.290) | copy-start | bytes 9220
  298.4 114.8 %copy-start.48 = (f32[768]{0:T(1024)}, f32[768]{0:T(1024)S(1)}, u32[]{:S(2)}) copy-start(f32[768]{0:T(1024)S(1)} %get-tuple-element.289) | copy-start | bytes 9220
  300.4 112.8 %copy-start.32 = (f32[1024]{0:T(1024)}, f32[1024]{0:T(1024)S(1)}, u32[]{:S(2)}) copy-start(f32[1024]{0:T(1024)S(1)} %broadcast_multiply_fusion.1) | copy-start | bytes 12292
  302.5 110.7 %copy-start.42 = (f32[1024]{0:T(1024)}, f32[1024]{0:T(1024)S(1)}, u32[]{:S(2)}) copy-start(f32[1024]{0:T(1024)S(1)} %fusion.118) | copy-start | bytes 12292
  303.1 90.4 %copy-start.34 = (f32[1024]{0:T(1024)}, f32[1024]{0:T(1024)S(1)}, u32[]{:S(2)}) copy-start(f32[1024]{0:T(1024)S(1)} %get-tuple-element.377) | copy-start | bytes 12292
  303.1 90.4 %copy-start.36 = (f32[1024]{0:T(1024)}, f32[1024]{0:T(1024)S(1)}, u32[]{:S(2)}) copy-start(f32[1024]{0:T(1024)S(1)} %get-tuple-element.378) | copy-start | bytes 12292
  381.8 4.9 copy-start.1
  389.7 3.9 copy-start.15
  393.5 7.8 copy-start.17
  537.0 7.0 copy-start.14
  541.0 43.9 %copy-start.4 = (f32[1024,768]{0,1:T(8,128)}, f32[1024,768]{0,1:T(8,128)S(1)}, u32[]{:S(2)}) copy-start(f32[1024,768]{0,1:T(8,128)S(1)} %get-tuple-element.370) | copy-start | bytes 9437188
  615.4 245.2 %reduce-scatter.6.cloned.1.call-start = ((), (), s32[]{:S(2)}) async-start(), calls=%async_computation.4 | async-start | bytes 5898240 | tf_op jit(solution)/shard_map/reduce_scatter | solution.py:252
  640.2 3.9 copy-start.5
  640.2 4.7 copy-start.8
  647.4 4.4 copy-start.23
  666.3 242.7 %reduce-scatter.4.cloned.1.call-start = ((), (), s32[]{:S(2)}) async-start(), calls=%async_computation.3 | async-start | bytes 5898240 | tf_op jit(solution)/shard_map/reduce_scatter | solution.py:249
  667.0 159.3 %copy-start.29 = (f32[12,32]{1,0:T(8,128)S(1)}, f32[12,32]{1,0:T(8,128)}, u32[]{:S(2)}) copy-start(f32[12,32]{1,0:T(8,128)} %copy-done.28) | copy-start | bytes 4612
  667.0 159.3 %copy-start.31 = (f32[12,32]{1,0:T(8,128)S(1)}, f32[12,32]{1,0:T(8,128)}, u32[]{:S(2)}) copy-start(f32[12,32]{1,0:T(8,128)} %copy-done.30) | copy-start | bytes 4612
  667.0 159.3 %copy-start.35 = (f32[1024]{0:T(1024)S(1)}, f32[1024]{0:T(1024)}, u32[]{:S(2)}) copy-start(f32[1024]{0:T(1024)} %copy-done.34) | copy-start | bytes 12292
  667.0 159.3 %copy-start.37 = (f32[1024]{0:T(1024)S(1)}, f32[1024]{0:T(1024)}, u32[]{:S(2)}) copy-start(f32[1024]{0:T(1024)} %copy-done.36) | copy-start | bytes 12292
  826.3 12.3 %copy-start.18 = (f32[12,1024,64]{1,2,0:T(8,128)S(1)}, f32[12,1024,64]{1,2,0:T(8,128)}, u32[]{:S(2)}) copy-start(f32[12,1024,64]{1,2,0:T(8,128)} %get-tuple-element.104) | copy-start | bytes 9437188
  838.3 2.5 copy-start.16
  838.5 17.7 %copy-start.25 = (bf16[1024,12,64]{0,2,1:T(8,128)(2,1)}, bf16[1024,12,64]{0,2,1:T(8,128)(2,1)S(1)}, u32[]{:S(2)}) copy-start(bf16[1024,12,64]{0,2,1:T(8,128)(2,1)S(1)} %get-tuple-element.342) | copy-start | bytes 4718596
  850.5 4.1 copy-start.26
  850.5 2.4 copy-start.10
  850.5 2.4 copy-start.33
  860.3 286.7 %all-reduce.11.cloned.1.call-start = ((), (), s32[]{:S(2)}) async-start(), calls=%async_computation.6 | async-start | bytes 14155776 | tf_op jit(solution)/shard_map/psum | solution.py:260
  914.4 5.1 copy-start.47
  932.5 3.3 copy-start.27
  935.7 2.8 copy-start.3
  935.8 2.8 copy-start.11
  938.6 3.2 copy-start.45
  947.5 5.5 copy-start.46
  951.0 50.0 %copy-start.39 = (f32[14,768]{1,0:T(8,128)S(1)}, f32[14,768]{1,0:T(8,128)}, u32[]{:S(2)}) copy-start(f32[14,768]{1,0:T(8,128)} %param.22) | copy-start | bytes 129028
  1170.1 5.0 copy-start.19
  1177.5 8.9 copy-start.56
  (15 other events, 26.7 us)
Sparse Core Ops, SparseCore 0:
  292.4 89.3 all-gather.2
  615.5 47.9 reduce-scatter.7
  666.4 48.3 reduce-scatter.5
  860.4 48.5 reduce-scatter.3
  914.5 232.5 all-reduce.10
where the time goes:
time: 1220 us; the launch traced here: 1200 us
  matrix products  359 us (29%)
  blocking collectives  323 us (26%)
  waiting for transfers between devices  271 us (22%)
  local copies, waits for them, and re-layouts  115 us (9%)
  other arithmetic  115 us (9%)
  between operations  18.4 us (2%)
    psum x1, blocking collectives, local(): blocks = lax.psum(owned_blocks, 'dp')  278 us
    psum x1, waiting for transfers between devices, local(): reduced = lax.psum(grad_stack, 'dp')  144 us
    all_gather x1, waiting for transfers between devices, local(): every_block = lax.all_gather(blocks_low[None], 'mlp', axis=0, tiled=True)  78.7 us
    dot_general x24, matrix products, head_scores(): jnp.dot(query_head, key_head.T, preferred_element_type=jnp.float32)  52.2 us
    reduce_scatter x1, waiting for transfers between devices, local(): lax.psum_scatter(attention_grads.astype(jnp.bfloat16), 'mlp', scatter_dim...  48.4 us
    psum x1, blocking collectives, local(): vector_sum = lax.psum(local_vectors, ('dp', 'mlp'))  45.1 us
    dot_general x1, matrix products, local(): jnp.einsum('td,mde->tme', norm_two_low, up_weight, preferred_element_type...  40.9 us
    dot_general x12, matrix products, head_forward(): jnp.dot(weights_low, value_head, preferred_element_type=jnp.float32)  35.5 us
  transfers between devices with their start and end apart: 5, of which 3 were waited for; matrix products, arithmetic and copies ran while one was open for 24% of the time, Pallas kernels for 0%

commit v1 on v0

--- a/solution.py
+++ b/solution.py
@@ -1,3 +1,4 @@
+import functools
 import math
 import jax
 import jax.numpy as jnp
@@ -12,6 +13,16 @@
 RATE_MATRIX = 0.04
 RATE_VECTOR = 0.02
 MASKED_SCORE = -1e30
+
+
+def match_column(u_in, axis_tag):
+    big = tuple((u_in for _ in range(lax.axis_size(axis_tag))))
+    b_now = jnp.stack(big, axis=0)
+    tile_out = lax.all_to_all(b_now, axis_tag, 0, 0)
+    return jnp.concatenate(tile_out, axis=0)
+
+
+serve_panel = functools.partial(match_column, axis_tag="mlp")
 
 
 def layer_norm(values, gain_row, shift_row):
@@ -94,7 +105,7 @@
     up_rows = vectors[8 : 8 + groups_mlp]
     down_bias = vectors[8 + groups_mlp]
     freq_row = vectors[9 + groups_mlp]
-    every_block = lax.all_gather(blocks_low[None], "mlp", axis=0, tiled=True)
+    every_block = serve_panel(blocks_low[None])
     attention_weights = every_block[:, 0]
     up_weight = every_block[:, 1]
     down_weight = every_block[:, 2]

time: 1220 us -> 1300 us (1.066)
  waiting for transfers between devices: 271 us -> 334 us
  local copies, waits for them, and re-layouts: 115 us -> 129 us
    all_to_all x0 -> x1, waiting for transfers between devices: none -> 145 us  [match_column(): tile_out = lax.all_to_all(b_now, axis_tag, 0, 0)]
    all_gather x1 -> x0, waiting for transfers between devices: 78.7 us -> none  [local(): every_block = lax.all_gather(blocks_low[None], 'mlp', axis=0, tiled=True)]
    unnamed x121 -> x123, local copies, waits for them, and re-layouts: 33.5 us -> 36.1 us
  transfers between devices with their start and end apart: 5 -> 5, of which waited for: 3 -> 3; matrix products, arithmetic and copies ran while one was open for 24% -> 22% of each run, Pallas kernels for 0% -> 0%
where the time goes in v1:
time: 1300 us; the launch traced here: 1280 us
  matrix products  355 us (27%)
  waiting for transfers between devices  334 us (26%)
  blocking collectives  323 us (25%)
  local copies, waits for them, and re-layouts  129 us (10%)
  other arithmetic  114 us (9%)
  between operations  18.4 us (1%)
    psum x1, blocking collectives, local(): blocks = lax.psum(owned_blocks, 'dp')  278 us
    all_to_all x1, waiting for transfers between devices, match_column(): tile_out = lax.all_to_all(b_now, axis_tag, 0, 0)  145 us
    psum x1, waiting for transfers between devices, local(): reduced = lax.psum(grad_stack, 'dp')  144 us
    dot_general x24, matrix products, head_scores(): jnp.dot(query_head, key_head.T, preferred_element_type=jnp.float32)  52.3 us
    reduce_scatter x1, waiting for transfers between devices, local(): lax.psum_scatter(attention_grads.astype(jnp.bfloat16), 'mlp', scatter_dim...  45.3 us
    psum x1, blocking collectives, local(): vector_sum = lax.psum(local_vectors, ('dp', 'mlp'))  45.2 us
    dot_general x1, matrix products, local(): jnp.einsum('td,mde->tme', norm_two_low, up_weight, preferred_element_type...  40.9 us
    unnamed x123, local copies, waits for them, and re-layouts  36.1 us
  transfers between devices with their start and end apart: 5, of which 3 were waited for; matrix products, arithmetic and copies ran while one was open for 22% of the time, Pallas kernels for 0%

profile of v1, /device:TPU:0, one launch (start us, length us, event | category | flops | bytes accessed | tf_op | source)
XLA Modules:
  0.0 1281.9 jit_solution(8047192213544388597)
XLA Ops:
  8.7 5.2 broadcast_select_fusion
  13.9 278.3 %all-reduce.12 = bf16[3,768,768]{2,1,0:T(8,128)(2,1)} all-reduce(f32[3,768,768]{2,1,0:T(8,128)} %broadcast_select_fusion), channel_id=1, replica_groups=mesh['dp'=8,'mlp'=4] {'dp'}, use_global_device_ids=true, to_apply=%region_2.3 | all-reduce | flops 1769472 | bytes 10616832 | tf_op jit(solution)/shard_map/psum | solution.py:103
  292.2 6.4 stack.45
  298.6 6.5 all-to-all-start
  315.4 144.6 %all-to-all-done = bf16[4,1,3,768,768]{4,3,2,1,0:T(8,128)(2,1)} async-done(((bf16[4,1,3,768,768]{4,3,2,1,0:T(8,128)(2,1)}), bf16[4,1,3,768,768]{4,3,2,1,0:T(8,128)(2,1)}, u32[]{:S(2)}, u32[]{:S(2)}) %all-to-all-start) | async-done | bytes 14155808 | tf_op jit(solution)/shard_map/all_to_all | solution.py:21
  460.1 7.4 copy.134
  475.9 7.7 subtract_convert_fusion
  484.8 4.1 copy.100
  491.4 4.1 copy.101
  495.5 4.5 add_convert_fusion.4
  500.0 4.1 copy.99
  504.1 85.7 %while.32 = (s32[]{:T(128)}, bf16[12,1024,64]{1,2,0:T(8,128)(2,1)}, f32[12,1024]{1,0:T(8,128)}, bf16[12,1024,64]{2,1,0:T(8,128)(2,1)}, bf16[12,1024,64]{2,1,0:T(...) while((s32[]{:T(128)}, bf16[12,1024,64]{1,2,0:T(8,128)(2,1)}, ...), condition=%wide.region_8.9_spmd.clone.clone, body=%wide.region_5.8_spmd.clone.sunk.clone | while | flops 284163072 | bytes 13695065 | solution.py:152
  521.2 3.0 fusion.195
  535.5 3.0 fusion.195
  556.9 3.0 fusion.195
  571.2 3.0 fusion.195
  589.8 10.2 fusion.64
  600.0 12.7 copy.129
  612.7 6.6 copy.102
  619.3 4.0 fusion.140
  626.3 40.9 %convert_reduce_fusion = (f32[3072]{0:T(1024)}, bf16[1024,3072]{1,0:T(8,128)(2,1)}, f32[1024,3072]{1,0:T(8,128)}, f32[1024,3072]{1,0:T(8,128)}) fusion(f32[1024,3072]{1,0:T(8,128)S(1)} %copy-done.15, f32[3072]{0:T(1024)S(1)} %add.236, bf16[3072,768]{1,0:T(8,128)(2,1)} %bitcast.298, f32[1024,768]{0,1:T(8,128)S(1)} %get-tuple-element.370, ...), kind=kOutput, calls=%fused_computation.59 | convolution fusion | flops 5071696896 | bytes 51943424 | tf_op jit(solution)/shard_map/td,mde->tme/dot_general | solution.py:161
  667.3 12.8 %multiply_convert_fusion.1 = bf16[1024,3072]{1,0:T(8,128)(2,1)} fusion(f32[1024,3072]{1,0:T(8,128)} %get-tuple-element.336, f32[1024,3072]{1,0:T(8,128)} %get-tuple-element.371, f32[3072]{0:T(1024)S(1)} %add.236), kind=kLoop, calls=%fused_computation.61 | loop fusion | flops 12582912 | bytes 31469568 | tf_op jit(solution)/shard_map/convert_element_type | solution.py:167
  680.1 8.6 copy.131
  688.7 9.0 convolution_convert_fusion
  700.4 9.0 copy.132
  709.4 9.8 fusion.141
  719.2 3.5 copy.108
  722.7 4.0 multiply_reduce_fusion.1
  730.0 4.4 convolution_convert_fusion.1
  734.4 4.1 copy.109
  738.5 10.3 convert_bitcast_fusion
  749.5 159.3 %while.33 = (s32[]{:T(128)}, f32[12,1024,64]{1,2,0:T(8,128)}, f32[12,1024,64]{1,2,0:T(8,128)}, bf16[12,1024,64]{1,2,0:T(8,128)(2,1)}, bf16[12,1024,64]{2,1,0:T(8...) while((s32[]{:T(128)}, f32[12,1024,64]{1,2,0:T(8,128)}, ...), condition=%wide.region_15.16_spmd.clone.clone, body=%wide.region_13.15_spmd.clone.sunk.clone | while | flops 681704448 | bytes 34112624 | solution.py:216
  908.9 12.0 multiply_add_fusion.1
  923.3 7.8 multiply_add_fusion
  943.2 45.3 %reduce-scatter.4.cloned.1.call-done = bf16[1,768,768]{2,1,0:T(8,128)(2,1)} async-done(((bf16[4,768,768]{2,1,0:T(8,128)(2,1)}), bf16[1,768,768]{2,1,0:T(8,128)(2,1)}) %reduce-scatter.4.cloned.1.call-update) | async-done | bytes 1179664 | tf_op jit(solution)/shard_map/reduce_scatter | solution.py:260
  988.6 5.3 maximum_convert_fusion
  999.0 10.5 fusion.75
  1012.0 3.3 fusion.114
  1018.2 3.2 fusion.133
  1023.8 3.3 convert_reduce_fusion.2
  1027.0 3.6 copy.121
  1035.4 45.2 %psum.23 = f32[14,768]{1,0:T(8,128)S(1)} all-reduce(f32[14,768]{1,0:T(8,128)S(1)} %concatenate.21), channel_id=1, replica_groups=mesh['dp'=8,'mlp'=4] {'dp','mlp'}, use_global_device_ids=true, to_apply=%region_39.40 | all-reduce | flops 10752 | bytes 86016 | tf_op jit(solution)/shard_map/psum | solution.py:255
  1082.7 143.9 %all-reduce.11.cloned.1.call-done = f32[3,768,768]{2,1,0:T(8,128)} async-done(((f32[3,768,768]{2,1,0:T(8,128)}), f32[3,768,768]{2,1,0:T(8,128)}) %all-reduce.11.cloned.1.call-update) | async-done | bytes 7077904 | tf_op jit(solution)/shard_map/psum | solution.py:271
  1226.6 13.6 %fusion.79 = f32[768,768]{1,0:T(8,128)S(1)} fusion(f32[1,1,768,768]{3,2,1,0:T(8,128)} %param.29, f32[3,768,768]{2,1,0:T(8,128)} %all-reduce.11.cloned.1.call-done, s32[]{:T(128)S(6)} %select_n.95, pred[]{:T(512)S(6)} %and.13), kind=kOutput, calls=%fused_computation.125 | convolution fusion | flops 5436407808 | bytes 7077893 | tf_op jit(solution)/shard_map/dot_general | solution.py:286
  1240.2 8.7 multiply_reduce_fusion.4
  1249.7 5.0 fusion.76
  1257.1 8.9 fusion.84
  1265.9 9.2 fusion.82
  (334 shorter events, 299.3 us)
Async XLA Ops:
  7.2 1233.0 %copy-start = (f32[1,1,768,768]{3,2,1,0:T(8,128)S(1)}, f32[1,1,768,768]{3,2,1,0:T(8,128)}, u32[]{:S(2)}) copy-start(f32[1,1,768,768]{3,2,1,0:T(8,128)} %param.30) | copy-start | bytes 7077892
  298.6 161.5 %all-to-all-start = ((bf16[4,1,3,768,768]{4,3,2,1,0:T(8,128)(2,1)}), bf16[4,1,3,768,768]{4,3,2,1,0:T(8,128)(2,1)}, u32[]{:S(2)}, u32[]{:S(2)}) async-start(bf16[4,1,3,768,768]{4,3,2,1,0:T(8,128)(2,1)} %stack.45), calls=%async_computation | async-start | bytes 28311552 | tf_op jit(solution)/shard_map/all_to_all | solution.py:21
  305.1 638.1 %reduce-scatter.8.cloned.1.call-start = ((), (), s32[]{:S(2)}) async-start(), calls=%async_computation.6 | async-start | bytes 5898240 | tf_op jit(solution)/shard_map/reduce_scatter | solution.py:266
  306.5 3.8 copy-start.39
  306.5 4.0 slice-start
  306.5 4.0 copy-start.21
  306.5 4.0 copy-start.54
  306.5 4.0 copy-start.55
  307.7 7.7 copy-start.51
  307.7 7.7 copy-start.52
  310.4 165.4 %copy-start.29 = (f32[12,32]{1,0:T(8,128)}, f32[12,32]{1,0:T(8,128)S(1)}, u32[]{:S(2)}) copy-start(f32[12,32]{1,0:T(8,128)S(1)} %mul.390) | copy-start | bytes 4612
  310.5 165.4 %copy-start.31 = (f32[12,32]{1,0:T(8,128)}, f32[12,32]{1,0:T(8,128)S(1)}, u32[]{:S(2)}) copy-start(f32[12,32]{1,0:T(8,128)S(1)} %mul.385) | copy-start | bytes 4612
  311.2 184.3 %copy-start.41 = (f32[768]{0:T(1024)}, f32[768]{0:T(1024)S(1)}, u32[]{:S(2)}) copy-start(f32[768]{0:T(1024)S(1)} %get-tuple-element.290) | copy-start | bytes 9220
  311.2 184.3 %copy-start.49 = (f32[768]{0:T(1024)}, f32[768]{0:T(1024)S(1)}, u32[]{:S(2)}) copy-start(f32[768]{0:T(1024)S(1)} %get-tuple-element.289) | copy-start | bytes 9220
  312.9 182.6 %copy-start.33 = (f32[1024]{0:T(1024)}, f32[1024]{0:T(1024)S(1)}, u32[]{:S(2)}) copy-start(f32[1024]{0:T(1024)S(1)} %broadcast_multiply_fusion.1) | copy-start | bytes 12292
  314.8 180.7 %copy-start.43 = (f32[1024]{0:T(1024)}, f32[1024]{0:T(1024)S(1)}, u32[]{:S(2)}) copy-start(f32[1024]{0:T(1024)S(1)} %fusion.118) | copy-start | bytes 12292
  315.4 160.4 %copy-start.35 = (f32[1024]{0:T(1024)}, f32[1024]{0:T(1024)S(1)}, u32[]{:S(2)}) copy-start(f32[1024]{0:T(1024)S(1)} %get-tuple-element.377) | copy-start | bytes 12292
  315.4 160.4 %copy-start.37 = (f32[1024]{0:T(1024)}, f32[1024]{0:T(1024)S(1)}, u32[]{:S(2)}) copy-start(f32[1024]{0:T(1024)S(1)} %get-tuple-element.378) | copy-start | bytes 12292
  467.5 6.7 copy-start.4
  467.5 2.5 copy-start.1
  471.7 4.2 copy-start.16
  475.8 7.8 copy-start.18
  619.3 7.0 copy-start.15
  623.3 43.9 %copy-start.5 = (f32[1024,768]{0,1:T(8,128)}, f32[1024,768]{0,1:T(8,128)S(1)}, u32[]{:S(2)}) copy-start(f32[1024,768]{0,1:T(8,128)S(1)} %get-tuple-element.370) | copy-start | bytes 9437188
  697.7 245.5 %reduce-scatter.6.cloned.1.call-start = ((), (), s32[]{:S(2)}) async-start(), calls=%async_computation.5 | async-start | bytes 5898240 | tf_op jit(solution)/shard_map/reduce_scatter | solution.py:263
  722.7 4.0 copy-start.6
  722.7 4.8 copy-start.9
  730.0 4.4 copy-start.24
  748.8 239.7 %reduce-scatter.4.cloned.1.call-start = ((), (), s32[]{:S(2)}) async-start(), calls=%async_computation.4 | async-start | bytes 5898240 | tf_op jit(solution)/shard_map/reduce_scatter | solution.py:260
  749.5 159.4 %copy-start.30 = (f32[12,32]{1,0:T(8,128)S(1)}, f32[12,32]{1,0:T(8,128)}, u32[]{:S(2)}) copy-start(f32[12,32]{1,0:T(8,128)} %copy-done.29) | copy-start | bytes 4612
  749.5 159.4 %copy-start.32 = (f32[12,32]{1,0:T(8,128)S(1)}, f32[12,32]{1,0:T(8,128)}, u32[]{:S(2)}) copy-start(f32[12,32]{1,0:T(8,128)} %copy-done.31) | copy-start | bytes 4612
  749.5 159.4 %copy-start.36 = (f32[1024]{0:T(1024)S(1)}, f32[1024]{0:T(1024)}, u32[]{:S(2)}) copy-start(f32[1024]{0:T(1024)} %copy-done.35) | copy-start | bytes 12292
  749.5 159.4 %copy-start.38 = (f32[1024]{0:T(1024)S(1)}, f32[1024]{0:T(1024)}, u32[]{:S(2)}) copy-start(f32[1024]{0:T(1024)} %copy-done.37) | copy-start | bytes 12292
  908.9 12.3 copy-start.19
  920.9 2.5 copy-start.17
  921.1 17.7 %copy-start.26 = (bf16[1024,12,64]{0,2,1:T(8,128)(2,1)}, bf16[1024,12,64]{0,2,1:T(8,128)(2,1)S(1)}, u32[]{:S(2)}) copy-start(bf16[1024,12,64]{0,2,1:T(8,128)(2,1)S(1)} %get-tuple-element.342) | copy-start | bytes 4718596
  933.0 4.1 copy-start.27
  933.0 2.4 copy-start.34
  942.9 283.7 %all-reduce.11.cloned.1.call-start = ((), (), s32[]{:S(2)}) async-start(), calls=%async_computation.7 | async-start | bytes 14155776 | tf_op jit(solution)/shard_map/psum | solution.py:271
  993.9 5.1 copy-start.48
  1012.0 3.3 copy-start.28
  1015.3 2.8 copy-start.3
  1015.3 2.8 copy-start.12
  1018.1 3.2 copy-start.46
  1027.0 5.5 copy-start.47
  1030.6 50.0 %copy-start.40 = (f32[14,768]{1,0:T(8,128)S(1)}, f32[14,768]{1,0:T(8,128)}, u32[]{:S(2)}) copy-start(f32[14,768]{1,0:T(8,128)} %param.22) | copy-start | bytes 129028
  1249.7 5.0 copy-start.20
  1257.1 8.9 copy-start.57
  (16 other events, 29.2 us)
Sparse Core Ops, SparseCore 0:
  697.9 45.3 reduce-scatter.7
  749.0 45.4 reduce-scatter.5
  943.0 45.4 reduce-scatter.3
  994.1 232.5 all-reduce.10
